TPU v7x, 32 devices: a whole 2x2x4 slice. The times are simulated.
32 devices in a mesh: parts: 2 (over y), panel: 4 (over z), zone: 2 (over x), rhs: 2 (over core).
Axes of the slice: x: 2, y: 2, z: 4, core: 2. Of those that a mesh axis runs over, the one named last changes fastest.
Arguments:
- source: bfloat16 [4, 4096, 512], P(('parts', 'zone'), 'panel', 'rhs'), parts along dimension 0, may hold values from -6 to 6
- inverse: bfloat16 [4, 4096, 4096], P(('parts', 'zone'), 'panel'), parts along dimension 0, may hold values from -0.09375 to 0.09375
- coupling: bfloat16 [4, 4096, 4096], P(('parts', 'zone'), 'panel'), parts along dimension 0, may hold values from -0.078125 to 0.078125
Outputs:
- eliminated: bfloat16 [4, 4096, 512], P(('parts', 'zone'), 'panel', 'rhs'), parts along dimension 0
There are 2 independent parts, one for each index of `parts`. A program takes and returns all parts, laid end to end along the dimension named above; each array names one. Nothing has to cross between parts.
All inputs are finite; a program needn't handle non-finite values.
Results may differ from a plain program's by a relative error of at most 0.013.
Values may be sent and summed in bfloat16 or wider, within the bound.
No kernel may reach another device: no remote copies, remote signals or barrier semaphores. Data moves between devices by JAX's collectives and lax.ppermute only.
A program may use at most 64 MiB of HBM per device.

v0:
```python
import jax
import jax.numpy as jnp
from jax import lax
from jax.sharding import PartitionSpec as P


def from_behind(block, axis, distance):
    devices = range(lax.axis_size(axis))
    route = [(i - distance, i) for i in devices if i - distance in devices]
    return lax.ppermute(block, axis, route)


def local(source, inverse, coupling):
    inverse_block = inverse[0]
    coupling_block = coupling[0]
    local_rhs = source[0]
    row_count = local_rhs.shape[0]
    local_cols = local_rhs.shape[1]
    batch_count = 4
    group_cols = local_cols // batch_count
    zone_count = lax.axis_size("zone")
    zone_index = lax.axis_index("zone")
    total_steps = zone_count + batch_count - 1
    reduced = jnp.dot(
        inverse_block,
        lax.all_gather(local_rhs, "panel", axis=0, tiled=True),
        preferred_element_type=jnp.float32,
    )

    def advance(position, carried):
        previous, result = carried
        micro_index = position - zone_index
        is_live = jnp.logical_and(micro_index >= 0, micro_index < batch_count)
        clipped = jnp.clip(micro_index, 0, batch_count - 1)
        start_col = clipped * group_cols
        incoming = from_behind(previous, "zone", 1)
        initial = lax.dynamic_slice_in_dim(reduced, start_col, group_cols, 1)
        combined = initial - jnp.dot(
            coupling_block,
            lax.all_gather(incoming, "panel", axis=0, tiled=True),
            preferred_element_type=jnp.float32,
        )
        rounded = combined.astype(jnp.bfloat16)
        current = lax.dynamic_slice_in_dim(result, start_col, group_cols, 1)
        updated = lax.dynamic_update_slice_in_dim(
            result, jnp.where(is_live, rounded, current), start_col, 1
        )
        return (rounded, updated)

    starting = (
        jnp.zeros((row_count, group_cols), jnp.bfloat16),
        jnp.zeros((row_count, local_cols), jnp.bfloat16),
    )
    _, result = lax.fori_loop(0, total_steps, advance, starting)
    return result[None]


def solution(mesh):
    in_specs = (
        P(("parts", "zone"), "panel", "rhs"),
        P(("parts", "zone"), "panel", None),
        P(("parts", "zone"), "panel", None),
    )
    out_specs = P(("parts", "zone"), "panel", "rhs")
    return jax.shard_map(local, mesh=mesh, in_specs=in_specs, out_specs=out_specs, check_vma=False)
```

profile of v0, /device:TPU:0, one launch (start us, length us, event | category | flops | bytes accessed | tf_op | source)
XLA Modules:
  0.0 211.5 jit_solution(5797174708042044751)
XLA Ops:
  6.5 0.0 all-gather.3.cloned.1.call-start
  6.5 0.7 all-gather.3.cloned.1.call-update
  7.3 50.3 %all-gather.3.cloned.1.call-done = bf16[1,4096,256]{2,1,0:T(8,128)(2,1)} async-done(((bf16[1,1024,256]{2,1,0:T(8,128)(2,1)}), bf16[1,4096,256]{2,1,0:T(8,128)(2,1)}) %all-gather.3.cloned.1.call-update) | async-done | bytes 2097168 | tf_op jit(solution)/shard_map/all_gather | solution.py:26
  57.6 6.3 %fusion.1 = f32[1024,256]{0,1:T(8,128)S(1)} fusion(bf16[1,1024,4096]{2,1,0:T(8,128)(2,1)} %param.6, bf16[1,4096,256]{2,1,0:T(8,128)(2,1)} %all-gather.3.cloned.1.call-done), kind=kOutput, calls=%fused_computation.4 | convolution fusion | flops 2147483648 | bytes 11534336 | tf_op jit(solution)/shard_map/dot_general | solution.py:24
  64.0 0.1 broadcast_in_dim.10
  64.0 139.6 %while.16 = (s32[]{:T(128)}, bf16[1024,64]{0,1:T(8,128)(2,1)S(1)}, bf16[1024,256]{0,1:T(8,128)(2,1)S(1)}, s32[]{:T(128)}, f32[1024,256]{0,1:T(8,128)S(1)}, /*ind...) while((s32[]{:T(128)}, bf16[1024,64]{0,1:T(8,128)(2,1)S(1)}, ...), condition=%wide.region_1.2_spmd.clone, body=%wide.region_0.1_spmd.clone.sunk | while | flops 537133056 | bytes 11010323 | solution.py:54
  64.0 3.4 %collective-permute-start = (bf16[1024,64]{0,1:T(8,128)(2,1)S(1)}, bf16[1024,64]{0,1:T(8,128)(2,1)S(1)}, u32[]{:S(2)}, u32[]{:S(2)}) collective-permute-start(bf16[1024,64]{0,1:T(8,128)(2,1)S(1)} %broadcast_select_fusion.2), channel_id=1, source_target_pairs={{0,2},{1,3},{4,6},{5,7},{8,10},{9,11},{12,14},{13,15},{16,18},{17,... | collective-permute-start | bytes 393224 | tf_op jit(solution)/shard_map/while/body/eval_jaxpr/ppermute | solution.py:10
  67.5 2.7 %collective-permute-done = bf16[1024,64]{0,1:T(8,128)(2,1)S(1)} collective-permute-done((bf16[1024,64]{0,1:T(8,128)(2,1)S(1)}, bf16[1024,64]{0,1:T(8,128)(2,1)S(1)}, u32[]{:S(2)}, u32[]{:S(2)}) %collective-permute-start) | collective-permute-done | bytes 131104 | tf_op jit(solution)/shard_map/while/body/eval_jaxpr/ppermute | solution.py:10
  70.2 16.1 %all_gather.13 = bf16[4096,64]{0,1:T(8,128)(2,1)S(1)} all-gather(bf16[1024,64]{0,1:T(8,128)(2,1)S(1)} %collective-permute-done), channel_id=1, replica_groups=mesh['parts'=2,'panel'=4,'zone'=2,'rhs'=2] {'panel'}, dimensions={0}, use_global_device_ids=true | all-gather | bytes 655360 | tf_op jit(solution)/shard_map/while/body/eval_jaxpr/all_gather | solution.py:40
  86.2 6.0 %select_dynamic-update-slice_fusion.2 = (bf16[1024,256]{0,1:T(8,128)(2,1)S(1)}, bf16[1024,64]{0,1:T(8,128)(2,1)S(1)}) fusion(bf16[1024,256]{0,1:T(8,128)(2,1)S(1)} %get-tuple-element.211, s32[]{:T(128)S(6)} %select_n.35, pred[]{:T(512)S(6)} %and.10, bf16[1024,4096]{1,0:T(8,128)(2,1)} %get-tuple-element.226, bf16[4096,64]{0,1:T(8,128)(2,1)S(1)} %all_gather.13, ...), kind=kOutput, calls=%fused_computation.2.clone.1 | convolution fusion | flops 537067520 | bytes 9568261 | tf_op jit(solution)/shard_map/while/body/eval_jaxpr/dot_general | solution.py:38
  92.3 4.4 %collective-permute-start = (bf16[1024,64]{0,1:T(8,128)(2,1)S(1)}, bf16[1024,64]{0,1:T(8,128)(2,1)S(1)}, u32[]{:S(2)}, u32[]{:S(2)}) collective-permute-start(bf16[1024,64]{0,1:T(8,128)(2,1)S(1)} %broadcast_select_fusion.2), channel_id=1, source_target_pairs={{0,2},{1,3},{4,6},{5,7},{8,10},{9,11},{12,14},{13,15},{16,18},{17,... | collective-permute-start | bytes 393224 | tf_op jit(solution)/shard_map/while/body/eval_jaxpr/ppermute | solution.py:10
  96.7 2.5 %collective-permute-done = bf16[1024,64]{0,1:T(8,128)(2,1)S(1)} collective-permute-done((bf16[1024,64]{0,1:T(8,128)(2,1)S(1)}, bf16[1024,64]{0,1:T(8,128)(2,1)S(1)}, u32[]{:S(2)}, u32[]{:S(2)}) %collective-permute-start) | collective-permute-done | bytes 131104 | tf_op jit(solution)/shard_map/while/body/eval_jaxpr/ppermute | solution.py:10
  99.2 15.8 %all_gather.13 = bf16[4096,64]{0,1:T(8,128)(2,1)S(1)} all-gather(bf16[1024,64]{0,1:T(8,128)(2,1)S(1)} %collective-permute-done), channel_id=1, replica_groups=mesh['parts'=2,'panel'=4,'zone'=2,'rhs'=2] {'panel'}, dimensions={0}, use_global_device_ids=true | all-gather | bytes 655360 | tf_op jit(solution)/shard_map/while/body/eval_jaxpr/all_gather | solution.py:40
  115.0 6.0 %select_dynamic-update-slice_fusion.2 = (bf16[1024,256]{0,1:T(8,128)(2,1)S(1)}, bf16[1024,64]{0,1:T(8,128)(2,1)S(1)}) fusion(bf16[1024,256]{0,1:T(8,128)(2,1)S(1)} %get-tuple-element.211, s32[]{:T(128)S(6)} %select_n.35, pred[]{:T(512)S(6)} %and.10, bf16[1024,4096]{1,0:T(8,128)(2,1)} %get-tuple-element.226, bf16[4096,64]{0,1:T(8,128)(2,1)S(1)} %all_gather.13, ...), kind=kOutput, calls=%fused_computation.2.clone.1 | convolution fusion | flops 537067520 | bytes 9568261 | tf_op jit(solution)/shard_map/while/body/eval_jaxpr/dot_general | solution.py:38
  121.1 4.0 %collective-permute-start = (bf16[1024,64]{0,1:T(8,128)(2,1)S(1)}, bf16[1024,64]{0,1:T(8,128)(2,1)S(1)}, u32[]{:S(2)}, u32[]{:S(2)}) collective-permute-start(bf16[1024,64]{0,1:T(8,128)(2,1)S(1)} %broadcast_select_fusion.2), channel_id=1, source_target_pairs={{0,2},{1,3},{4,6},{5,7},{8,10},{9,11},{12,14},{13,15},{16,18},{17,... | collective-permute-start | bytes 393224 | tf_op jit(solution)/shard_map/while/body/eval_jaxpr/ppermute | solution.py:10
  125.1 2.5 %collective-permute-done = bf16[1024,64]{0,1:T(8,128)(2,1)S(1)} collective-permute-done((bf16[1024,64]{0,1:T(8,128)(2,1)S(1)}, bf16[1024,64]{0,1:T(8,128)(2,1)S(1)}, u32[]{:S(2)}, u32[]{:S(2)}) %collective-permute-start) | collective-permute-done | bytes 131104 | tf_op jit(solution)/shard_map/while/body/eval_jaxpr/ppermute | solution.py:10
  127.6 14.7 %all_gather.13 = bf16[4096,64]{0,1:T(8,128)(2,1)S(1)} all-gather(bf16[1024,64]{0,1:T(8,128)(2,1)S(1)} %collective-permute-done), channel_id=1, replica_groups=mesh['parts'=2,'panel'=4,'zone'=2,'rhs'=2] {'panel'}, dimensions={0}, use_global_device_ids=true | all-gather | bytes 655360 | tf_op jit(solution)/shard_map/while/body/eval_jaxpr/all_gather | solution.py:40
  142.4 6.0 %select_dynamic-update-slice_fusion.2 = (bf16[1024,256]{0,1:T(8,128)(2,1)S(1)}, bf16[1024,64]{0,1:T(8,128)(2,1)S(1)}) fusion(bf16[1024,256]{0,1:T(8,128)(2,1)S(1)} %get-tuple-element.211, s32[]{:T(128)S(6)} %select_n.35, pred[]{:T(512)S(6)} %and.10, bf16[1024,4096]{1,0:T(8,128)(2,1)} %get-tuple-element.226, bf16[4096,64]{0,1:T(8,128)(2,1)S(1)} %all_gather.13, ...), kind=kOutput, calls=%fused_computation.2.clone.1 | convolution fusion | flops 537067520 | bytes 9568261 | tf_op jit(solution)/shard_map/while/body/eval_jaxpr/dot_general | solution.py:38
  148.4 4.4 %collective-permute-start = (bf16[1024,64]{0,1:T(8,128)(2,1)S(1)}, bf16[1024,64]{0,1:T(8,128)(2,1)S(1)}, u32[]{:S(2)}, u32[]{:S(2)}) collective-permute-start(bf16[1024,64]{0,1:T(8,128)(2,1)S(1)} %broadcast_select_fusion.2), channel_id=1, source_target_pairs={{0,2},{1,3},{4,6},{5,7},{8,10},{9,11},{12,14},{13,15},{16,18},{17,... | collective-permute-start | bytes 393224 | tf_op jit(solution)/shard_map/while/body/eval_jaxpr/ppermute | solution.py:10
  152.8 2.5 %collective-permute-done = bf16[1024,64]{0,1:T(8,128)(2,1)S(1)} collective-permute-done((bf16[1024,64]{0,1:T(8,128)(2,1)S(1)}, bf16[1024,64]{0,1:T(8,128)(2,1)S(1)}, u32[]{:S(2)}, u32[]{:S(2)}) %collective-permute-start) | collective-permute-done | bytes 131104 | tf_op jit(solution)/shard_map/while/body/eval_jaxpr/ppermute | solution.py:10
  155.3 14.7 %all_gather.13 = bf16[4096,64]{0,1:T(8,128)(2,1)S(1)} all-gather(bf16[1024,64]{0,1:T(8,128)(2,1)S(1)} %collective-permute-done), channel_id=1, replica_groups=mesh['parts'=2,'panel'=4,'zone'=2,'rhs'=2] {'panel'}, dimensions={0}, use_global_device_ids=true | all-gather | bytes 655360 | tf_op jit(solution)/shard_map/while/body/eval_jaxpr/all_gather | solution.py:40
  170.0 6.0 %select_dynamic-update-slice_fusion.2 = (bf16[1024,256]{0,1:T(8,128)(2,1)S(1)}, bf16[1024,64]{0,1:T(8,128)(2,1)S(1)}) fusion(bf16[1024,256]{0,1:T(8,128)(2,1)S(1)} %get-tuple-element.211, s32[]{:T(128)S(6)} %select_n.35, pred[]{:T(512)S(6)} %and.10, bf16[1024,4096]{1,0:T(8,128)(2,1)} %get-tuple-element.226, bf16[4096,64]{0,1:T(8,128)(2,1)S(1)} %all_gather.13, ...), kind=kOutput, calls=%fused_computation.2.clone.1 | convolution fusion | flops 537067520 | bytes 9568261 | tf_op jit(solution)/shard_map/while/body/eval_jaxpr/dot_general | solution.py:38
  176.1 4.4 %collective-permute-start = (bf16[1024,64]{0,1:T(8,128)(2,1)S(1)}, bf16[1024,64]{0,1:T(8,128)(2,1)S(1)}, u32[]{:S(2)}, u32[]{:S(2)}) collective-permute-start(bf16[1024,64]{0,1:T(8,128)(2,1)S(1)} %broadcast_select_fusion.2), channel_id=1, source_target_pairs={{0,2},{1,3},{4,6},{5,7},{8,10},{9,11},{12,14},{13,15},{16,18},{17,... | collective-permute-start | bytes 393224 | tf_op jit(solution)/shard_map/while/body/eval_jaxpr/ppermute | solution.py:10
  180.5 2.5 %collective-permute-done = bf16[1024,64]{0,1:T(8,128)(2,1)S(1)} collective-permute-done((bf16[1024,64]{0,1:T(8,128)(2,1)S(1)}, bf16[1024,64]{0,1:T(8,128)(2,1)S(1)}, u32[]{:S(2)}, u32[]{:S(2)}) %collective-permute-start) | collective-permute-done | bytes 131104 | tf_op jit(solution)/shard_map/while/body/eval_jaxpr/ppermute | solution.py:10
  182.9 14.6 %all_gather.13 = bf16[4096,64]{0,1:T(8,128)(2,1)S(1)} all-gather(bf16[1024,64]{0,1:T(8,128)(2,1)S(1)} %collective-permute-done), channel_id=1, replica_groups=mesh['parts'=2,'panel'=4,'zone'=2,'rhs'=2] {'panel'}, dimensions={0}, use_global_device_ids=true | all-gather | bytes 655360 | tf_op jit(solution)/shard_map/while/body/eval_jaxpr/all_gather | solution.py:40
  197.6 6.0 %select_dynamic-update-slice_fusion.2 = (bf16[1024,256]{0,1:T(8,128)(2,1)S(1)}, bf16[1024,64]{0,1:T(8,128)(2,1)S(1)}) fusion(bf16[1024,256]{0,1:T(8,128)(2,1)S(1)} %get-tuple-element.211, s32[]{:T(128)S(6)} %select_n.35, pred[]{:T(512)S(6)} %and.10, bf16[1024,4096]{1,0:T(8,128)(2,1)} %get-tuple-element.226, bf16[4096,64]{0,1:T(8,128)(2,1)S(1)} %all_gather.13, ...), kind=kOutput, calls=%fused_computation.2.clone.1 | convolution fusion | flops 537067520 | bytes 9568261 | tf_op jit(solution)/shard_map/while/body/eval_jaxpr/dot_general | solution.py:38
  203.6 1.0 copy.5
  (6 shorter events, 0.1 us)
Async XLA Ops:
  6.5 51.1 %all-gather.3.cloned.1.call-start = ((), (), s32[]{:S(2)}) async-start(), calls=%async_computation | async-start | bytes 2621440 | tf_op jit(solution)/shard_map/all_gather | solution.py:26
  64.0 6.1 %collective-permute-start = (bf16[1024,64]{0,1:T(8,128)(2,1)S(1)}, bf16[1024,64]{0,1:T(8,128)(2,1)S(1)}, u32[]{:S(2)}, u32[]{:S(2)}) collective-permute-start(bf16[1024,64]{0,1:T(8,128)(2,1)S(1)} %broadcast_select_fusion.2), channel_id=1, source_target_pairs={{0,2},{1,3},{4,6},{5,7},{8,10},{9,11},{12,14},{13,15},{16,18},{17,... | collective-permute-start | bytes 393224 | tf_op jit(solution)/shard_map/while/body/eval_jaxpr/ppermute | solution.py:10
  92.3 6.9 %collective-permute-start = (bf16[1024,64]{0,1:T(8,128)(2,1)S(1)}, bf16[1024,64]{0,1:T(8,128)(2,1)S(1)}, u32[]{:S(2)}, u32[]{:S(2)}) collective-permute-start(bf16[1024,64]{0,1:T(8,128)(2,1)S(1)} %broadcast_select_fusion.2), channel_id=1, source_target_pairs={{0,2},{1,3},{4,6},{5,7},{8,10},{9,11},{12,14},{13,15},{16,18},{17,... | collective-permute-start | bytes 393224 | tf_op jit(solution)/shard_map/while/body/eval_jaxpr/ppermute | solution.py:10
  121.1 6.6 %collective-permute-start = (bf16[1024,64]{0,1:T(8,128)(2,1)S(1)}, bf16[1024,64]{0,1:T(8,128)(2,1)S(1)}, u32[]{:S(2)}, u32[]{:S(2)}) collective-permute-start(bf16[1024,64]{0,1:T(8,128)(2,1)S(1)} %broadcast_select_fusion.2), channel_id=1, source_target_pairs={{0,2},{1,3},{4,6},{5,7},{8,10},{9,11},{12,14},{13,15},{16,18},{17,... | collective-permute-start | bytes 393224 | tf_op jit(solution)/shard_map/while/body/eval_jaxpr/ppermute | solution.py:10
  148.4 6.9 %collective-permute-start = (bf16[1024,64]{0,1:T(8,128)(2,1)S(1)}, bf16[1024,64]{0,1:T(8,128)(2,1)S(1)}, u32[]{:S(2)}, u32[]{:S(2)}) collective-permute-start(bf16[1024,64]{0,1:T(8,128)(2,1)S(1)} %broadcast_select_fusion.2), channel_id=1, source_target_pairs={{0,2},{1,3},{4,6},{5,7},{8,10},{9,11},{12,14},{13,15},{16,18},{17,... | collective-permute-start | bytes 393224 | tf_op jit(solution)/shard_map/while/body/eval_jaxpr/ppermute | solution.py:10
  176.1 6.9 %collective-permute-start = (bf16[1024,64]{0,1:T(8,128)(2,1)S(1)}, bf16[1024,64]{0,1:T(8,128)(2,1)S(1)}, u32[]{:S(2)}, u32[]{:S(2)}) collective-permute-start(bf16[1024,64]{0,1:T(8,128)(2,1)S(1)} %broadcast_select_fusion.2), channel_id=1, source_target_pairs={{0,2},{1,3},{4,6},{5,7},{8,10},{9,11},{12,14},{13,15},{16,18},{17,... | collective-permute-start | bytes 393224 | tf_op jit(solution)/shard_map/while/body/eval_jaxpr/ppermute | solution.py:10
Sparse Core Ops, SparseCore 0:
  8.9 48.6 all-gather.2
where the time goes:
time: 212 us; the launch traced here: 211 us
  blocking collectives  75.9 us (36%)
  waiting for transfers between devices  63.7 us (30%)
  matrix products  36.6 us (17%)
  starting transfers between devices  20.5 us (10%)
  between operations  13.4 us (6%)
    all_gather x5, blocking collectives, advance(): lax.all_gather(incoming, 'panel', axis=0, tiled=True)  75.9 us
    all_gather x1, waiting for transfers between devices, local(): lax.all_gather(local_rhs, 'panel', axis=0, tiled=True)  50.3 us
    dot_general x5, matrix products, advance(): jnp.dot(coupling_block, lax.all_gather(incoming, 'panel', axis=0, tiled=T...  30.2 us
    ppermute x5, starting transfers between devices, from_behind(): return lax.ppermute(block, axis, route)  20.5 us
    ppermute x5, waiting for transfers between devices, from_behind(): return lax.ppermute(block, axis, route)  12.6 us
    dot_general x1, matrix products, local(): jnp.dot(inverse_block, lax.all_gather(local_rhs, 'panel', axis=0, tiled=T...  6.34 us
  transfers between devices with their start and end apart: 6, of which 6 were waited for; matrix products, arithmetic and copies ran while one was open for 0% of the time, Pallas kernels for 0%

commit v1 on v0

--- a/solution.py
+++ b/solution.py
@@ -1,7 +1,35 @@
+import functools
 import jax
 import jax.numpy as jnp
 from jax import lax
 from jax.sharding import PartitionSpec as P
+
+
+def view_the_teams(piece_in, array_axis):
+    moved = lax.axis_size("panel")
+    reached = lax.axis_index("panel")
+    ready, back, placed = (moved, reached, piece_in.shape[array_axis])
+    pieces_in = []
+    for rr, b in enumerate(piece_in.shape):
+        pieces_in.append(b * ready if rr == array_axis else b)
+    next_value = jnp.zeros(pieces_in, piece_in.dtype)
+    y_new = lax.dynamic_update_slice_in_dim(next_value, piece_in, back * placed, axis=array_axis)
+    nth = 1
+    while nth < ready:
+        kept_rows = []
+        rr = 0
+        while rr < ready:
+            kept_rows.append((rr, (rr + 1) % ready))
+            rr += 1
+        piece_in = lax.ppermute(piece_in, "panel", kept_rows)
+        y_new = lax.dynamic_update_slice_in_dim(
+            y_new, piece_in, (back - nth) % ready * placed, axis=array_axis
+        )
+        nth += 1
+    return y_new
+
+
+group_ratios_in = functools.partial(view_the_teams, array_axis=0)
 
 
 def from_behind(block, axis, distance):
@@ -21,11 +49,7 @@
     zone_count = lax.axis_size("zone")
     zone_index = lax.axis_index("zone")
     total_steps = zone_count + batch_count - 1
-    reduced = jnp.dot(
-        inverse_block,
-        lax.all_gather(local_rhs, "panel", axis=0, tiled=True),
-        preferred_element_type=jnp.float32,
-    )
+    reduced = jnp.dot(inverse_block, group_ratios_in(local_rhs), preferred_element_type=jnp.float32)
 
     def advance(position, carried):
         previous, result = carried

time: 212 us -> 191 us (0.901)
  between operations: 13.4 us -> 0.07 us
  waiting for transfers between devices: 63.7 us -> 55.2 us
  starting transfers between devices: 20.5 us -> 23.6 us
  blocking collectives: 75.9 us -> 73.6 us
    all_gather x1 -> x0, waiting for transfers between devices: 50.3 us -> none  [local(): lax.all_gather(local_rhs, 'panel', axis=0, tiled=True)]
    ppermute x0 -> x3, waiting for transfers between devices: none -> 42.8 us  [view_the_teams(): piece_in = lax.ppermute(piece_in, 'panel', kept_rows)]
    ppermute x0 -> x3, starting transfers between devices: none -> 3.03 us  [view_the_teams(): piece_in = lax.ppermute(piece_in, 'panel', kept_rows)]
    all_gather x5, blocking collectives: 75.9 us -> 73.6 us  [advance(): lax.all_gather(incoming, 'panel', axis=0, tiled=True)]
  transfers between devices with their start and end apart: 6 -> 8, of which waited for: 6 -> 8; matrix products, arithmetic and copies ran while one was open for 0% -> 0% of each run, Pallas kernels for 0% -> 0%
where the time goes in v1:
time: 191 us; the launch traced here: 190 us
  blocking collectives  73.6 us (39%)
  waiting for transfers between devices  55.2 us (29%)
  matrix products  36 us (19%)
  starting transfers between devices  23.6 us (12%)
    all_gather x5, blocking collectives, advance(): lax.all_gather(incoming, 'panel', axis=0, tiled=True)  73.6 us
    ppermute x3, waiting for transfers between devices, view_the_teams(): piece_in = lax.ppermute(piece_in, 'panel', kept_rows)  42.8 us
    dot_general x5, matrix products, advance(): jnp.dot(coupling_block, lax.all_gather(incoming, 'panel', axis=0, tiled=T...  30.2 us
    ppermute x5, starting transfers between devices, from_behind(): return lax.ppermute(block, axis, route)  20.6 us
    ppermute x5, waiting for transfers between devices, from_behind(): return lax.ppermute(block, axis, route)  12.4 us
    dot_general x1, matrix products, local(): jnp.dot(inverse_block, group_ratios_in(local_rhs), preferred_element_type...  5.76 us
  transfers between devices with their start and end apart: 8, of which 8 were waited for; matrix products, arithmetic and copies ran while one was open for 0% of the time, Pallas kernels for 0%

profile of v1, /device:TPU:0, one launch (start us, length us, event | category | flops | bytes accessed | tf_op | source)
XLA Modules:
  0.0 190.1 jit_solution(9714795842926822278)
XLA Ops:
  0.0 0.0 copy-start
  0.0 3.0 %collective-permute-start.1 = (bf16[1024,256]{1,0:T(8,128)(2,1)}, bf16[1024,256]{1,0:T(8,128)(2,1)S(1)}, u32[]{:S(2)}, u32[]{:S(2)}) collective-permute-start(bf16[1024,256]{1,0:T(8,128)(2,1)} %bitcast.19), channel_id=1, source_target_pairs={{0,4},{4,8},{8,12},{12,0},{1,5},{5,9},{9,13},{13,1},{2,6},{6,10},{... | collective-permute-start | bytes 1572872 | tf_op jit(solution)/shard_map/ppermute | solution.py:24
  3.0 14.2 %collective-permute-done.1 = bf16[1024,256]{1,0:T(8,128)(2,1)S(1)} collective-permute-done((bf16[1024,256]{1,0:T(8,128)(2,1)}, bf16[1024,256]{1,0:T(8,128)(2,1)S(1)}, u32[]{:S(2)}, u32[]{:S(2)}) %collective-permute-start.1) | collective-permute-done | bytes 524320 | tf_op jit(solution)/shard_map/ppermute | solution.py:24
  17.3 0.0 collective-permute-start.2
  17.3 14.9 %collective-permute-done.2 = bf16[1024,256]{1,0:T(8,128)(2,1)S(1)} collective-permute-done((bf16[1024,256]{1,0:T(8,128)(2,1)S(1)}, bf16[1024,256]{1,0:T(8,128)(2,1)S(1)}, u32[]{:S(2)}, u32[]{:S(2)}) %collective-permute-start.2) | collective-permute-done | bytes 524320 | tf_op jit(solution)/shard_map/ppermute | solution.py:24
  32.2 0.0 collective-permute-start.3
  32.2 0.1 broadcast_in_dim.14
  32.3 0.0 copy-done
  32.5 13.7 %collective-permute-done.3 = bf16[1024,256]{1,0:T(8,128)(2,1)S(1)} collective-permute-done((bf16[1024,256]{1,0:T(8,128)(2,1)S(1)}, bf16[1024,256]{1,0:T(8,128)(2,1)S(1)}, u32[]{:S(2)}, u32[]{:S(2)}) %collective-permute-start.3) | collective-permute-done | bytes 524320 | tf_op jit(solution)/shard_map/ppermute | solution.py:24
  46.2 5.8 %fusion.3 = f32[1024,256]{0,1:T(8,128)S(1)} fusion(bf16[4096,256]{1,0:T(8,128)(2,1)S(1)} %constant_dynamic-update-slice_fusion, bf16[1,1024,4096]{2,1,0:T(8,128)(2,1)} %param.6), kind=kOutput, calls=%fused_computation.6 | convolution fusion | flops 2147483648 | bytes 11534336 | tf_op jit(solution)/shard_map/dot_general | solution.py:52
  52.0 0.1 broadcast_in_dim.13
  52.0 137.1 %while.16 = (s32[]{:T(128)}, bf16[1024,64]{0,1:T(8,128)(2,1)S(1)}, bf16[1024,256]{0,1:T(8,128)(2,1)S(1)}, s32[]{:T(128)}, f32[1024,256]{0,1:T(8,128)S(1)}, /*ind...) while((s32[]{:T(128)}, bf16[1024,64]{0,1:T(8,128)(2,1)S(1)}, ...), condition=%wide.region_1.2_spmd.clone, body=%wide.region_0.1_spmd.clone.sunk | while | flops 537133056 | bytes 11010323 | solution.py:78
  52.1 3.1 %collective-permute-start = (bf16[1024,64]{0,1:T(8,128)(2,1)S(1)}, bf16[1024,64]{0,1:T(8,128)(2,1)S(1)}, u32[]{:S(2)}, u32[]{:S(2)}) collective-permute-start(bf16[1024,64]{0,1:T(8,128)(2,1)S(1)} %broadcast_select_fusion.2), channel_id=1, source_target_pairs={{0,2},{1,3},{4,6},{5,7},{8,10},{9,11},{12,14},{13,15},{16,18},{17,... | collective-permute-start | bytes 393224 | tf_op jit(solution)/shard_map/while/body/eval_jaxpr/ppermute | solution.py:38
  55.1 2.5 %collective-permute-done = bf16[1024,64]{0,1:T(8,128)(2,1)S(1)} collective-permute-done((bf16[1024,64]{0,1:T(8,128)(2,1)S(1)}, bf16[1024,64]{0,1:T(8,128)(2,1)S(1)}, u32[]{:S(2)}, u32[]{:S(2)}) %collective-permute-start) | collective-permute-done | bytes 131104 | tf_op jit(solution)/shard_map/while/body/eval_jaxpr/ppermute | solution.py:38
  57.6 14.8 %all_gather.9 = bf16[4096,64]{0,1:T(8,128)(2,1)S(1)} all-gather(bf16[1024,64]{0,1:T(8,128)(2,1)S(1)} %collective-permute-done), channel_id=1, replica_groups=mesh['parts'=2,'panel'=4,'zone'=2,'rhs'=2] {'panel'}, dimensions={0}, use_global_device_ids=true | all-gather | bytes 655360 | tf_op jit(solution)/shard_map/while/body/eval_jaxpr/all_gather | solution.py:64
  72.4 6.0 %select_dynamic-update-slice_fusion.2 = (bf16[1024,256]{0,1:T(8,128)(2,1)S(1)}, bf16[1024,64]{0,1:T(8,128)(2,1)S(1)}) fusion(bf16[1024,256]{0,1:T(8,128)(2,1)S(1)} %get-tuple-element.205, s32[]{:T(128)S(6)} %select_n.69, pred[]{:T(512)S(6)} %and.27, bf16[1024,4096]{1,0:T(8,128)(2,1)} %get-tuple-element.220, bf16[4096,64]{0,1:T(8,128)(2,1)S(1)} %all_gather.9, ...), kind=kOutput, calls=%fused_computation.2.clone.1 | convolution fusion | flops 537067520 | bytes 9568261 | tf_op jit(solution)/shard_map/while/body/eval_jaxpr/dot_general | solution.py:62
  78.5 4.4 %collective-permute-start = (bf16[1024,64]{0,1:T(8,128)(2,1)S(1)}, bf16[1024,64]{0,1:T(8,128)(2,1)S(1)}, u32[]{:S(2)}, u32[]{:S(2)}) collective-permute-start(bf16[1024,64]{0,1:T(8,128)(2,1)S(1)} %broadcast_select_fusion.2), channel_id=1, source_target_pairs={{0,2},{1,3},{4,6},{5,7},{8,10},{9,11},{12,14},{13,15},{16,18},{17,... | collective-permute-start | bytes 393224 | tf_op jit(solution)/shard_map/while/body/eval_jaxpr/ppermute | solution.py:38
  83.0 2.5 %collective-permute-done = bf16[1024,64]{0,1:T(8,128)(2,1)S(1)} collective-permute-done((bf16[1024,64]{0,1:T(8,128)(2,1)S(1)}, bf16[1024,64]{0,1:T(8,128)(2,1)S(1)}, u32[]{:S(2)}, u32[]{:S(2)}) %collective-permute-start) | collective-permute-done | bytes 131104 | tf_op jit(solution)/shard_map/while/body/eval_jaxpr/ppermute | solution.py:38
  85.4 14.6 %all_gather.9 = bf16[4096,64]{0,1:T(8,128)(2,1)S(1)} all-gather(bf16[1024,64]{0,1:T(8,128)(2,1)S(1)} %collective-permute-done), channel_id=1, replica_groups=mesh['parts'=2,'panel'=4,'zone'=2,'rhs'=2] {'panel'}, dimensions={0}, use_global_device_ids=true | all-gather | bytes 655360 | tf_op jit(solution)/shard_map/while/body/eval_jaxpr/all_gather | solution.py:64
  100.1 6.0 %select_dynamic-update-slice_fusion.2 = (bf16[1024,256]{0,1:T(8,128)(2,1)S(1)}, bf16[1024,64]{0,1:T(8,128)(2,1)S(1)}) fusion(bf16[1024,256]{0,1:T(8,128)(2,1)S(1)} %get-tuple-element.205, s32[]{:T(128)S(6)} %select_n.69, pred[]{:T(512)S(6)} %and.27, bf16[1024,4096]{1,0:T(8,128)(2,1)} %get-tuple-element.220, bf16[4096,64]{0,1:T(8,128)(2,1)S(1)} %all_gather.9, ...), kind=kOutput, calls=%fused_computation.2.clone.1 | convolution fusion | flops 537067520 | bytes 9568261 | tf_op jit(solution)/shard_map/while/body/eval_jaxpr/dot_general | solution.py:62
  106.2 4.4 %collective-permute-start = (bf16[1024,64]{0,1:T(8,128)(2,1)S(1)}, bf16[1024,64]{0,1:T(8,128)(2,1)S(1)}, u32[]{:S(2)}, u32[]{:S(2)}) collective-permute-start(bf16[1024,64]{0,1:T(8,128)(2,1)S(1)} %broadcast_select_fusion.2), channel_id=1, source_target_pairs={{0,2},{1,3},{4,6},{5,7},{8,10},{9,11},{12,14},{13,15},{16,18},{17,... | collective-permute-start | bytes 393224 | tf_op jit(solution)/shard_map/while/body/eval_jaxpr/ppermute | solution.py:38
  110.6 2.5 %collective-permute-done = bf16[1024,64]{0,1:T(8,128)(2,1)S(1)} collective-permute-done((bf16[1024,64]{0,1:T(8,128)(2,1)S(1)}, bf16[1024,64]{0,1:T(8,128)(2,1)S(1)}, u32[]{:S(2)}, u32[]{:S(2)}) %collective-permute-start) | collective-permute-done | bytes 131104 | tf_op jit(solution)/shard_map/while/body/eval_jaxpr/ppermute | solution.py:38
  113.0 14.6 %all_gather.9 = bf16[4096,64]{0,1:T(8,128)(2,1)S(1)} all-gather(bf16[1024,64]{0,1:T(8,128)(2,1)S(1)} %collective-permute-done), channel_id=1, replica_groups=mesh['parts'=2,'panel'=4,'zone'=2,'rhs'=2] {'panel'}, dimensions={0}, use_global_device_ids=true | all-gather | bytes 655360 | tf_op jit(solution)/shard_map/while/body/eval_jaxpr/all_gather | solution.py:64
  127.7 6.0 %select_dynamic-update-slice_fusion.2 = (bf16[1024,256]{0,1:T(8,128)(2,1)S(1)}, bf16[1024,64]{0,1:T(8,128)(2,1)S(1)}) fusion(bf16[1024,256]{0,1:T(8,128)(2,1)S(1)} %get-tuple-element.205, s32[]{:T(128)S(6)} %select_n.69, pred[]{:T(512)S(6)} %and.27, bf16[1024,4096]{1,0:T(8,128)(2,1)} %get-tuple-element.220, bf16[4096,64]{0,1:T(8,128)(2,1)S(1)} %all_gather.9, ...), kind=kOutput, calls=%fused_computation.2.clone.1 | convolution fusion | flops 537067520 | bytes 9568261 | tf_op jit(solution)/shard_map/while/body/eval_jaxpr/dot_general | solution.py:62
  133.8 4.4 %collective-permute-start = (bf16[1024,64]{0,1:T(8,128)(2,1)S(1)}, bf16[1024,64]{0,1:T(8,128)(2,1)S(1)}, u32[]{:S(2)}, u32[]{:S(2)}) collective-permute-start(bf16[1024,64]{0,1:T(8,128)(2,1)S(1)} %broadcast_select_fusion.2), channel_id=1, source_target_pairs={{0,2},{1,3},{4,6},{5,7},{8,10},{9,11},{12,14},{13,15},{16,18},{17,... | collective-permute-start | bytes 393224 | tf_op jit(solution)/shard_map/while/body/eval_jaxpr/ppermute | solution.py:38
  138.2 2.5 %collective-permute-done = bf16[1024,64]{0,1:T(8,128)(2,1)S(1)} collective-permute-done((bf16[1024,64]{0,1:T(8,128)(2,1)S(1)}, bf16[1024,64]{0,1:T(8,128)(2,1)S(1)}, u32[]{:S(2)}, u32[]{:S(2)}) %collective-permute-start) | collective-permute-done | bytes 131104 | tf_op jit(solution)/shard_map/while/body/eval_jaxpr/ppermute | solution.py:38
  140.6 14.6 %all_gather.9 = bf16[4096,64]{0,1:T(8,128)(2,1)S(1)} all-gather(bf16[1024,64]{0,1:T(8,128)(2,1)S(1)} %collective-permute-done), channel_id=1, replica_groups=mesh['parts'=2,'panel'=4,'zone'=2,'rhs'=2] {'panel'}, dimensions={0}, use_global_device_ids=true | all-gather | bytes 655360 | tf_op jit(solution)/shard_map/while/body/eval_jaxpr/all_gather | solution.py:64
  155.3 6.0 %select_dynamic-update-slice_fusion.2 = (bf16[1024,256]{0,1:T(8,128)(2,1)S(1)}, bf16[1024,64]{0,1:T(8,128)(2,1)S(1)}) fusion(bf16[1024,256]{0,1:T(8,128)(2,1)S(1)} %get-tuple-element.205, s32[]{:T(128)S(6)} %select_n.69, pred[]{:T(512)S(6)} %and.27, bf16[1024,4096]{1,0:T(8,128)(2,1)} %get-tuple-element.220, bf16[4096,64]{0,1:T(8,128)(2,1)S(1)} %all_gather.9, ...), kind=kOutput, calls=%fused_computation.2.clone.1 | convolution fusion | flops 537067520 | bytes 9568261 | tf_op jit(solution)/shard_map/while/body/eval_jaxpr/dot_general | solution.py:62
  161.4 4.4 %collective-permute-start = (bf16[1024,64]{0,1:T(8,128)(2,1)S(1)}, bf16[1024,64]{0,1:T(8,128)(2,1)S(1)}, u32[]{:S(2)}, u32[]{:S(2)}) collective-permute-start(bf16[1024,64]{0,1:T(8,128)(2,1)S(1)} %broadcast_select_fusion.2), channel_id=1, source_target_pairs={{0,2},{1,3},{4,6},{5,7},{8,10},{9,11},{12,14},{13,15},{16,18},{17,... | collective-permute-start | bytes 393224 | tf_op jit(solution)/shard_map/while/body/eval_jaxpr/ppermute | solution.py:38
  165.8 2.5 %collective-permute-done = bf16[1024,64]{0,1:T(8,128)(2,1)S(1)} collective-permute-done((bf16[1024,64]{0,1:T(8,128)(2,1)S(1)}, bf16[1024,64]{0,1:T(8,128)(2,1)S(1)}, u32[]{:S(2)}, u32[]{:S(2)}) %collective-permute-start) | collective-permute-done | bytes 131104 | tf_op jit(solution)/shard_map/while/body/eval_jaxpr/ppermute | solution.py:38
  168.2 14.8 %all_gather.9 = bf16[4096,64]{0,1:T(8,128)(2,1)S(1)} all-gather(bf16[1024,64]{0,1:T(8,128)(2,1)S(1)} %collective-permute-done), channel_id=1, replica_groups=mesh['parts'=2,'panel'=4,'zone'=2,'rhs'=2] {'panel'}, dimensions={0}, use_global_device_ids=true | all-gather | bytes 655360 | tf_op jit(solution)/shard_map/while/body/eval_jaxpr/all_gather | solution.py:64
  183.0 6.0 %select_dynamic-update-slice_fusion.2 = (bf16[1024,256]{0,1:T(8,128)(2,1)S(1)}, bf16[1024,64]{0,1:T(8,128)(2,1)S(1)}) fusion(bf16[1024,256]{0,1:T(8,128)(2,1)S(1)} %get-tuple-element.205, s32[]{:T(128)S(6)} %select_n.69, pred[]{:T(512)S(6)} %and.27, bf16[1024,4096]{1,0:T(8,128)(2,1)} %get-tuple-element.220, bf16[4096,64]{0,1:T(8,128)(2,1)S(1)} %all_gather.9, ...), kind=kOutput, calls=%fused_computation.2.clone.1 | convolution fusion | flops 537067520 | bytes 9568261 | tf_op jit(solution)/shard_map/while/body/eval_jaxpr/dot_general | solution.py:62
  189.1 1.0 copy.4
  (10 shorter events, 0.2 us)
Async XLA Ops:
  0.0 32.3 %copy-start = (bf16[1,1024,256]{2,1,0:T(8,128)(2,1)S(1)}, bf16[1,1024,256]{2,1,0:T(8,128)(2,1)}, u32[]{:S(2)}) copy-start(bf16[1,1024,256]{2,1,0:T(8,128)(2,1)} %param.5) | copy-start | bytes 1572868
  0.0 17.3 %collective-permute-start.1 = (bf16[1024,256]{1,0:T(8,128)(2,1)}, bf16[1024,256]{1,0:T(8,128)(2,1)S(1)}, u32[]{:S(2)}, u32[]{:S(2)}) collective-permute-start(bf16[1024,256]{1,0:T(8,128)(2,1)} %bitcast.19), channel_id=1, source_target_pairs={{0,4},{4,8},{8,12},{12,0},{1,5},{5,9},{9,13},{13,1},{2,6},{6,10},{... | collective-permute-start | bytes 1572872 | tf_op jit(solution)/shard_map/ppermute | solution.py:24
  17.3 14.9 %collective-permute-start.2 = (bf16[1024,256]{1,0:T(8,128)(2,1)S(1)}, bf16[1024,256]{1,0:T(8,128)(2,1)S(1)}, u32[]{:S(2)}, u32[]{:S(2)}) collective-permute-start(bf16[1024,256]{1,0:T(8,128)(2,1)S(1)} %collective-permute-done.1), channel_id=1, source_target_pairs={{0,4},{4,8},{8,12},{12,0},{1,5},{5,9},{9,13},{13,1},{2,6},{6,10},{... | collective-permute-start | bytes 1572872 | tf_op jit(solution)/shard_map/ppermute | solution.py:24
  32.2 14.0 %collective-permute-start.3 = (bf16[1024,256]{1,0:T(8,128)(2,1)S(1)}, bf16[1024,256]{1,0:T(8,128)(2,1)S(1)}, u32[]{:S(2)}, u32[]{:S(2)}) collective-permute-start(bf16[1024,256]{1,0:T(8,128)(2,1)S(1)} %collective-permute-done.2), channel_id=1, source_target_pairs={{0,4},{4,8},{8,12},{12,0},{1,5},{5,9},{9,13},{13,1},{2,6},{6,10},{... | collective-permute-start | bytes 1572872 | tf_op jit(solution)/shard_map/ppermute | solution.py:24
  52.1 5.6 %collective-permute-start = (bf16[1024,64]{0,1:T(8,128)(2,1)S(1)}, bf16[1024,64]{0,1:T(8,128)(2,1)S(1)}, u32[]{:S(2)}, u32[]{:S(2)}) collective-permute-start(bf16[1024,64]{0,1:T(8,128)(2,1)S(1)} %broadcast_select_fusion.2), channel_id=1, source_target_pairs={{0,2},{1,3},{4,6},{5,7},{8,10},{9,11},{12,14},{13,15},{16,18},{17,... | collective-permute-start | bytes 393224 | tf_op jit(solution)/shard_map/while/body/eval_jaxpr/ppermute | solution.py:38
  78.5 6.9 %collective-permute-start = (bf16[1024,64]{0,1:T(8,128)(2,1)S(1)}, bf16[1024,64]{0,1:T(8,128)(2,1)S(1)}, u32[]{:S(2)}, u32[]{:S(2)}) collective-permute-start(bf16[1024,64]{0,1:T(8,128)(2,1)S(1)} %broadcast_select_fusion.2), channel_id=1, source_target_pairs={{0,2},{1,3},{4,6},{5,7},{8,10},{9,11},{12,14},{13,15},{16,18},{17,... | collective-permute-start | bytes 393224 | tf_op jit(solution)/shard_map/while/body/eval_jaxpr/ppermute | solution.py:38
  106.2 6.9 %collective-permute-start = (bf16[1024,64]{0,1:T(8,128)(2,1)S(1)}, bf16[1024,64]{0,1:T(8,128)(2,1)S(1)}, u32[]{:S(2)}, u32[]{:S(2)}) collective-permute-start(bf16[1024,64]{0,1:T(8,128)(2,1)S(1)} %broadcast_select_fusion.2), channel_id=1, source_target_pairs={{0,2},{1,3},{4,6},{5,7},{8,10},{9,11},{12,14},{13,15},{16,18},{17,... | collective-permute-start | bytes 393224 | tf_op jit(solution)/shard_map/while/body/eval_jaxpr/ppermute | solution.py:38
  133.8 6.9 %collective-permute-start = (bf16[1024,64]{0,1:T(8,128)(2,1)S(1)}, bf16[1024,64]{0,1:T(8,128)(2,1)S(1)}, u32[]{:S(2)}, u32[]{:S(2)}) collective-permute-start(bf16[1024,64]{0,1:T(8,128)(2,1)S(1)} %broadcast_select_fusion.2), channel_id=1, source_target_pairs={{0,2},{1,3},{4,6},{5,7},{8,10},{9,11},{12,14},{13,15},{16,18},{17,... | collective-permute-start | bytes 393224 | tf_op jit(solution)/shard_map/while/body/eval_jaxpr/ppermute | solution.py:38
  161.4 6.9 %collective-permute-start = (bf16[1024,64]{0,1:T(8,128)(2,1)S(1)}, bf16[1024,64]{0,1:T(8,128)(2,1)S(1)}, u32[]{:S(2)}, u32[]{:S(2)}) collective-permute-start(bf16[1024,64]{0,1:T(8,128)(2,1)S(1)} %broadcast_select_fusion.2), channel_id=1, source_target_pairs={{0,2},{1,3},{4,6},{5,7},{8,10},{9,11},{12,14},{13,15},{16,18},{17,... | collective-permute-start | bytes 393224 | tf_op jit(solution)/shard_map/while/body/eval_jaxpr/ppermute | solution.py:38
